TPU v7x, 32 devices: a whole 2x2x4 slice. The times are simulated.
32 devices in a mesh: dp: 8 (over z, y), tensor: 4 (over x, core).
Axes of the slice: x: 2, y: 2, z: 4, core: 2. Of those that a mesh axis runs over, the one named last changes fastest.
Arguments:
- tokens: bfloat16 [12288, 768], P('dp', 'tensor'), may hold values from -6 to 6
- cotangent: bfloat16 [12288, 768], P('dp', 'tensor'), may hold values from -6 to 6
- seq_start: int32 [12288], P('dp'), may hold values from 0 to 384, as said below
- row_place: int32 [8, 1536], P('dp'), may hold values from 0 to 1535, each once within a row
- qkv_weight: bfloat16 [3, 768, 768], P(None, None, 'tensor'), may hold values from -0.21875 to 0.21875
- qv_bias: bfloat16 [2, 768], P(None, 'tensor'), may hold values from -1.5 to 1.5
- out_weight: bfloat16 [768, 768], P('tensor'), may hold values from -0.875 to 0.875
- out_bias: bfloat16 [768], replicated, may hold values from -1.5 to 1.5
- first_gain: bfloat16 [768], replicated, may hold values from 0.5 to 1.5
- first_shift: bfloat16 [768], replicated, may hold values from -1.5 to 1.5
- up_weight: bfloat16 [2, 768, 3072], P(None, None, 'tensor'), may hold values from -0.21875 to 0.21875
- up_bias: bfloat16 [2, 3072], P(None, 'tensor'), may hold values from -1.5 to 1.5
- down_weight: bfloat16 [3072, 768], P('tensor'), may hold values from -0.15625 to 0.15625
- down_bias: bfloat16 [768], replicated, may hold values from -1.5 to 1.5
- second_gain: bfloat16 [768], replicated, may hold values from 0.5 to 1.5
- second_shift: bfloat16 [768], replicated, may hold values from -1.5 to 1.5
Outputs:
- layer_out: bfloat16 [12288, 768], P('dp', 'tensor')
- input_grad: bfloat16 [12288, 768], P('dp', 'tensor')
- qkv_grad: float32 [3, 768, 768], P(None, 'dp', 'tensor')
- qv_bias_grad: float32 [2, 768], P(None, 'tensor')
- out_grad: float32 [768, 768], P('tensor', 'dp')
- out_bias_grad: float32 [768], P('dp')
- first_gain_grad: float32 [768], P('dp')
- first_shift_grad: float32 [768], P('dp')
- up_grad: float32 [2, 768, 3072], P(None, 'dp', 'tensor')
- up_bias_grad: float32 [2, 3072], P(None, 'tensor')
- down_grad: float32 [3072, 768], P('tensor', 'dp')
- down_bias_grad: float32 [768], P('dp')
- second_gain_grad: float32 [768], P('dp')
- second_shift_grad: float32 [768], P('dp')
Inputs may be any that keep to these rules, and one draw needn't show every extreme that they name: seq_start of a token is the offset, within its aligned block of 512 packed rows, of the first token of its sequence; sequences are 128, 256 or 512 tokens long, begin at multiples of 128 and never cross a block. Each row of row_place is a permutation of 0 to 1535.
All inputs are finite; a program needn't handle non-finite values.
Results may differ from a plain program's by a relative error of at most 0.02.
The roundings to bfloat16 on the way count: a program that leaves them out, or rounds other values in their place, can miss the bound.
Values may be sent and summed in bfloat16 or wider, within the bound.
A program may use at most 128 MiB of HBM per device.

v0:
```python
import jax
import jax.numpy as jnp
from jax import lax
from jax.sharding import PartitionSpec as P

HEADS = 12
HEAD_DIM = 64
BLOCK = 512


def layer_norm(values, scale_row, shift_row):
    center = values - jnp.mean(values, axis=-1, keepdims=True)
    spread = jnp.mean(center * center, axis=-1, keepdims=True)
    return center * lax.rsqrt(spread + 1e-05) * scale_row + shift_row


def gated_unit(gate_part, value_part):
    return jax.nn.gelu(gate_part, approximate=False) * value_part


def alibi_terms(part_index, local_heads, block_rows):
    heads_idx = (part_index * local_heads + jnp.arange(local_heads)).astype(jnp.float32)
    slopes = 2.0 ** (-8.0 * (heads_idx + 1.0) / HEADS)
    position = jnp.arange(block_rows).astype(jnp.float32)
    distance = jnp.abs(position[:, None] - position[None, :])
    return -slopes[:, None, None] * distance[None]


def block_scores(queries, key_rows, alibi_bias, same_seq, score_scale):
    raw_scores = jnp.einsum(
        "bqhe,bkhe->bhqk", queries, key_rows, preferred_element_type=jnp.float32
    )
    scored = raw_scores * score_scale + alibi_bias[None]
    return jnp.where(same_seq[:, None], scored, -1e30)


def softmax_rows(scored):
    row_max = jnp.max(scored, axis=-1, keepdims=True)
    exponent = jnp.exp(scored - row_max)
    denominator = jnp.sum(exponent, axis=-1, keepdims=True)
    return (exponent / denominator, row_max + jnp.log(denominator))


def on_device(
    tokens,
    cotangent,
    seq_start,
    row_place,
    qkv_weight,
    qv_bias,
    out_weight,
    out_bias,
    first_gain,
    first_shift,
    up_weight,
    up_bias,
    down_weight,
    down_bias,
    second_gain,
    second_shift,
):
    arr_tokens, arr_cot = (
        lax.all_to_all(tokens, "dp", split_axis=0, concat_axis=0, tiled=True),
        lax.all_to_all(cotangent, "dp", split_axis=0, concat_axis=0, tiled=True),
    )
    wide_tokens, wide_cot = (
        lax.all_gather(arr_tokens, "tensor", axis=1, tiled=True),
        lax.all_gather(arr_cot, "tensor", axis=1, tiled=True),
    )
    slot_index = row_place[0]
    packed_in = jnp.zeros_like(wide_tokens).at[slot_index].set(wide_tokens)
    packed_cot = jnp.zeros_like(wide_cot).at[slot_index].set(wide_cot)
    row_count = packed_in.shape[0]
    columns = packed_in.shape[1]
    local_heads = qkv_weight.shape[2] // HEAD_DIM
    block_rows = BLOCK
    blocks = row_count // block_rows
    part_index = lax.axis_index("tensor")
    col_count = columns // lax.axis_size("tensor")
    score_scale = HEAD_DIM ** (-0.5)
    alibi_bias = alibi_terms(part_index, local_heads, block_rows)
    block_starts = seq_start.reshape(blocks, block_rows)
    same_seq = block_starts[:, :, None] == block_starts[:, None, :]
    bias_rows = jnp.stack([qv_bias[0], jnp.zeros_like(qv_bias[0]), qv_bias[1]]).astype(jnp.float32)
    projected = jnp.einsum("td,kde->kte", packed_in, qkv_weight, preferred_element_type=jnp.float32)
    qkv_rows = (projected + bias_rows[:, None, :]).astype(jnp.bfloat16)
    split_heads = qkv_rows.reshape(3, blocks, block_rows, local_heads, HEAD_DIM)
    queries = split_heads[0]
    key_rows = split_heads[1]
    value_rows = split_heads[2]
    attn_probs, log_total = softmax_rows(
        block_scores(queries, key_rows, alibi_bias, same_seq, score_scale)
    )
    context = jnp.einsum(
        "bhqk,bkhe->bqhe",
        attn_probs.astype(jnp.bfloat16),
        value_rows,
        preferred_element_type=jnp.float32,
    )
    context = context.reshape(row_count, local_heads * HEAD_DIM).astype(jnp.bfloat16)
    attn_part = jnp.dot(context, out_weight, preferred_element_type=jnp.float32)
    attended = lax.psum(attn_part, "tensor")
    hidden = packed_in.astype(jnp.float32) + (attended + out_bias.astype(jnp.float32))
    normed, first_pull = jax.vjp(
        layer_norm, hidden, first_gain.astype(jnp.float32), first_shift.astype(jnp.float32)
    )
    normed_low = normed.astype(jnp.bfloat16)
    lifted = jnp.einsum("td,kdf->ktf", normed_low, up_weight, preferred_element_type=jnp.float32)
    lifted = lifted + up_bias.astype(jnp.float32)[:, None, :]
    gated_val, gate_pull = jax.vjp(gated_unit, lifted[0], lifted[1])
    gated_low = gated_val.astype(jnp.bfloat16)
    ffn_part = jnp.dot(gated_low, down_weight, preferred_element_type=jnp.float32)
    ffn_out = lax.psum(ffn_part.astype(jnp.bfloat16), "tensor").astype(jnp.float32)
    mixed_rows = normed + (ffn_out + down_bias.astype(jnp.float32))
    result, second_pull = jax.vjp(
        layer_norm, mixed_rows, second_gain.astype(jnp.float32), second_shift.astype(jnp.float32)
    )
    grad_scale = (row_count * lax.axis_size("dp")) ** (-0.5)
    d_mixed, d_second_gain, d_second_shift = second_pull(packed_cot.astype(jnp.float32))
    d_mixed_low = d_mixed.astype(jnp.bfloat16)
    g_down = jnp.einsum("tf,td->fd", gated_low, d_mixed_low, preferred_element_type=jnp.float32)
    g_down_bias = jnp.sum(d_mixed, axis=0)
    d_gated = jnp.einsum("td,fd->tf", d_mixed_low, down_weight, preferred_element_type=jnp.float32)
    d_gate, d_value = gate_pull(d_gated)
    d_lifted = jnp.stack([d_gate, d_value]).astype(jnp.bfloat16)
    g_up = jnp.einsum("td,ktf->kdf", normed_low, d_lifted, preferred_element_type=jnp.float32)
    g_up_bias = jnp.sum(d_lifted, axis=1, dtype=jnp.float32)
    d_normed_part = jnp.einsum(
        "ktf,kdf->td", d_lifted, up_weight, preferred_element_type=jnp.float32
    )
    d_normed = d_mixed + lax.psum(d_normed_part.astype(jnp.bfloat16), "tensor").astype(jnp.float32)
    d_hidden, d_first_gain, d_first_shift = first_pull(d_normed)
    d_hidden_low = d_hidden.astype(jnp.bfloat16)
    g_out = jnp.einsum("te,td->ed", context, d_hidden_low, preferred_element_type=jnp.float32)
    g_out_bias = jnp.sum(d_hidden, axis=0)
    d_context = jnp.einsum(
        "td,ed->te", d_hidden_low, out_weight, preferred_element_type=jnp.float32
    )
    d_context = d_context.astype(jnp.bfloat16).reshape(blocks, block_rows, local_heads, HEAD_DIM)
    probs_back = jnp.exp(
        block_scores(queries, key_rows, alibi_bias, same_seq, score_scale) - log_total
    )
    d_probs = jnp.einsum(
        "bqhe,bkhe->bhqk", d_context, value_rows, preferred_element_type=jnp.float32
    )
    g_values = jnp.einsum(
        "bhqk,bqhe->bkhe",
        probs_back.astype(jnp.bfloat16),
        d_context,
        preferred_element_type=jnp.float32,
    )
    center_term = jnp.sum(probs_back * d_probs, axis=-1, keepdims=True)
    d_scores = (probs_back * (d_probs - center_term)).astype(jnp.bfloat16)
    g_queries = (
        jnp.einsum("bhqk,bkhe->bqhe", d_scores, key_rows, preferred_element_type=jnp.float32)
        * score_scale
    )
    g_keys = (
        jnp.einsum("bhqk,bqhe->bkhe", d_scores, queries, preferred_element_type=jnp.float32)
        * score_scale
    )
    d_qkv = jnp.stack([g_queries, g_keys, g_values]).reshape(3, row_count, local_heads * HEAD_DIM)
    d_qkv = d_qkv.astype(jnp.bfloat16)
    g_qkv = jnp.einsum("td,kte->kde", packed_in, d_qkv, preferred_element_type=jnp.float32)
    g_qv_bias = jnp.sum(jnp.stack([d_qkv[0], d_qkv[2]]), axis=1, dtype=jnp.float32)
    d_input_part = jnp.einsum("kte,kde->td", d_qkv, qkv_weight, preferred_element_type=jnp.float32)
    hidden_cols = lax.dynamic_slice_in_dim(d_hidden, part_index * col_count, col_count, 1)
    grad_cols = hidden_cols + lax.psum_scatter(
        d_input_part.astype(jnp.bfloat16), "tensor", scatter_dimension=1, tiled=True
    ).astype(jnp.float32)
    summed = (
        lax.psum_scatter(g_qkv * grad_scale, "dp", scatter_dimension=1, tiled=True),
        lax.psum_scatter(g_out * grad_scale, "dp", scatter_dimension=1, tiled=True),
        lax.psum_scatter(g_out_bias * grad_scale, "dp", scatter_dimension=0, tiled=True),
        lax.psum_scatter(d_first_gain * grad_scale, "dp", scatter_dimension=0, tiled=True),
        lax.psum_scatter(d_first_shift * grad_scale, "dp", scatter_dimension=0, tiled=True),
        lax.psum_scatter(g_up * grad_scale, "dp", scatter_dimension=1, tiled=True),
        lax.psum_scatter(g_down * grad_scale, "dp", scatter_dimension=1, tiled=True),
        lax.psum_scatter(g_down_bias * grad_scale, "dp", scatter_dimension=0, tiled=True),
        lax.psum_scatter(d_second_gain * grad_scale, "dp", scatter_dimension=0, tiled=True),
        lax.psum_scatter(d_second_shift * grad_scale, "dp", scatter_dimension=0, tiled=True),
    )
    qkv_grad, out_grad, out_bias_grad, first_gain_grad, first_shift_grad = (
        summed[0],
        summed[1],
        summed[2],
        summed[3],
        summed[4],
    )
    up_grad, down_grad, down_bias_grad, second_gain_grad, second_shift_grad = (
        summed[5],
        summed[6],
        summed[7],
        summed[8],
        summed[9],
    )
    qv_bias_grad, up_bias_grad = lax.psum((g_qv_bias * grad_scale, g_up_bias * grad_scale), "dp")
    layer_cols = lax.dynamic_slice_in_dim(result, part_index * col_count, col_count, 1)
    layer_back = layer_cols[slot_index].astype(jnp.bfloat16)
    grad_back = grad_cols[slot_index].astype(jnp.bfloat16)
    layer_out, input_grad = (
        lax.all_to_all(layer_back, "dp", split_axis=0, concat_axis=0, tiled=True),
        lax.all_to_all(grad_back, "dp", split_axis=0, concat_axis=0, tiled=True),
    )
    return (
        layer_out,
        input_grad,
        qkv_grad,
        qv_bias_grad,
        out_grad,
        out_bias_grad,
        first_gain_grad,
        first_shift_grad,
        up_grad,
        up_bias_grad,
        down_grad,
        down_bias_grad,
        second_gain_grad,
        second_shift_grad,
    )


def solution(mesh):
    return jax.shard_map(
        on_device,
        mesh=mesh,
        in_specs=(
            P("dp", "tensor"),
            P("dp", "tensor"),
            P("dp"),
            P("dp", None),
            P(None, None, "tensor"),
            P(None, "tensor"),
            P("tensor", None),
            P(),
            P(),
            P(),
            P(None, None, "tensor"),
            P(None, "tensor"),
            P("tensor", None),
            P(),
            P(),
            P(),
        ),
        out_specs=(
            P("dp", "tensor"),
            P("dp", "tensor"),
            P(None, "dp", "tensor"),
            P(None, "tensor"),
            P("tensor", "dp"),
            P("dp"),
            P("dp"),
            P("dp"),
            P(None, "dp", "tensor"),
            P(None, "tensor"),
            P("tensor", "dp"),
            P("dp"),
            P("dp"),
            P("dp"),
        ),
        check_vma=False,
    )
```

profile of v0, /device:TPU:0, one launch (start us, length us, event | category | flops | bytes accessed | tf_op | source)
XLA Modules:
  0.0 849.5 jit_solution(2268085062084630268)
XLA Ops:
  9.3 27.3 %all_to_all.42 = bf16[8,192,192]{1,2,0:T(8,128)(2,1)S(1)} all-to-all(bf16[8,192,192]{1,2,0:T(8,128)(2,1)S(1)} %copy.124), channel_id=1, replica_groups=mesh['dp'=8,'tensor'=4] {'dp'}, dimensions={0} | all-to-all | bytes 1179648 | tf_op jit(solution)/shard_map/all_to_all | solution.py:63
  42.5 19.2 %all-gather.3.cloned.1.call-done = bf16[1536,768]{0,1:T(8,128)(2,1)} async-done(((bf16[1536,192]{0,1:T(8,128)(2,1)}), bf16[1536,768]{0,1:T(8,128)(2,1)}) %all-gather.3.cloned.1.call-update) | async-done | bytes 2359312 | tf_op jit(solution)/shard_map/all_gather | solution.py:67
  66.0 9.8 %scatter_custom_fusion = bf16[1536,768]{1,0:T(8,128)(2,1)} fusion(s32[1536]{0:T(1024)S(1)} %fusion.70, bf16[1536,768]{1,0:T(8,128)(2,1)} %copy.126, bf16[]{:T(256)} %constant.46.clone.1), kind=kCustom, calls=%fused_computation.108 | custom fusion | bytes 2359808 | tf_op jit(solution)/shard_map/scatter | solution.py:71
  84.0 5.3 fusion.85
  103.2 5.5 all-to-all-start.2
  108.9 20.5 %all-to-all-done.2 = bf16[8,192,192]{1,2,0:T(8,128)(2,1)} async-done(((bf16[8,192,192]{1,2,0:T(8,128)(2,1)}), bf16[8,192,192]{1,2,0:T(8,128)(2,1)}, u32[]{:S(2)}, u32[]{:S(2)}) %all-to-all-start.2) | async-done | bytes 589856 | tf_op jit(solution)/shard_map/all_to_all | solution.py:64
  134.6 58.1 %all-reduce.13.cloned.1.call-done = f32[1536,768]{1,0:T(8,128)} async-done(((f32[1536,768]{1,0:T(8,128)}), f32[1536,768]{1,0:T(8,128)}) %all-reduce.13.cloned.1.call-update) | async-done | bytes 4718608 | tf_op jit(solution)/shard_map/psum | solution.py:102
  201.6 11.5 %multiply_convert_fusion.2 = (bf16[1536,768]{1,0:T(8,128)(2,1)S(1)}, f32[1536,768]{1,0:T(8,128)}) fusion(f32[2,1536,768]{2,1,0:T(8,128)S(1)} %add_bitcast_fusion), kind=kLoop, calls=%fused_computation.51 | loop fusion | flops 77856768 | bytes 16515072 | tf_op jit(solution)/shard_map/convert_element_type | solution.py:111
  223.4 10.0 %scatter_custom_fusion.1 = bf16[1536,768]{1,0:T(8,128)(2,1)} fusion(s32[1536]{0:T(1024)} %copy-done.29, bf16[1536,768]{1,0:T(8,128)(2,1)} %copy.135, bf16[]{:T(256)} %constant.46.clone.1), kind=kCustom, calls=%fused_computation.106 | custom fusion | bytes 2359808 | tf_op jit(solution)/shard_map/scatter | solution.py:72
  233.5 43.6 %all-reduce.15.cloned.1.call-done = bf16[1536,768]{1,0:T(8,128)(2,1)} async-done(((bf16[1536,768]{1,0:T(8,128)(2,1)}), bf16[1536,768]{1,0:T(8,128)(2,1)}) %all-reduce.15.cloned.1.call-update) | async-done | bytes 2359312 | tf_op jit(solution)/shard_map/psum | solution.py:113
  284.1 4.7 fusion.79
  288.9 7.1 fusion.36
  297.4 7.0 bitcast_convert_fusion.1
  305.2 55.0 %all-reduce.17.cloned.1.call-done = bf16[1536,768]{1,0:T(8,128)(2,1)} async-done(((bf16[1536,768]{1,0:T(8,128)(2,1)}), bf16[1536,768]{1,0:T(8,128)(2,1)}) %all-reduce.17.cloned.1.call-update) | async-done | bytes 2359312 | tf_op jit(solution)/shard_map/psum | solution.py:131
  360.3 6.5 multiply_reduce_fusion.1
  366.8 5.0 fusion.78
  376.6 5.3 fusion.48
  381.9 7.2 multiply_reduce_fusion
  389.1 11.2 %multiply_convert_fusion = bf16[3,3,512,512]{2,3,1,0:T(8,128)(2,1)} fusion(f32[3,3,512,512]{2,3,1,0:T(8,128)} %get-tuple-element.127, f32[3,3,512,512]{2,3,1,0:T(8,128)} %copy-done.2, f32[3,3,512]{2,1,0:T(4,128)S(1)} %get-tuple-element.126, f32[3,3,512]{2,1,0:T(4,128)S(1)} %copy-done.23), kind=kLoop, calls=%fused_computation.5 | loop fusion | flops 9437184 | bytes 23629824 | tf_op jit(solution)/shard_map/convert_element_type | solution.py:153
  416.8 4.6 fusion.31
  434.6 4.8 reshape.283
  439.6 9.6 %multiply_bitcast_fusion = f32[2,768,768]{1,2,0:T(8,128)} fusion(bf16[1,1536,768]{2,1,0:T(8,128)(2,1)} %get-tuple-element.114, bf16[1,1536,768]{2,1,0:T(8,128)(2,1)S(1)} %copy-done.19, f32[1536,768]{1,0:T(8,128)} %copy-done.3, f32[768]{0:T(1024)S(1)} %copy-done.34, f32[768]{0:T(1024)S(1)} %copy-done.28, f32[1536]{0:T(1024)S(1)} %fusion.68, ...), kind=kOutput, calls=%fused_computation.43 | convolution fusion | flops 3633315840 | bytes 14174208 | tf_op jit(solution)/shard_map/td,ktf->kdf/dot_general | solution.py:126
  449.2 8.3 copy.150
  459.1 6.0 convolution_multiply_fusion
  467.4 5.4 gather_fusion
  472.8 5.3 all-to-all-start.1
  482.4 17.3 %all-to-all-done.1 = bf16[8,192,192]{2,1,0:T(8,128)(2,1)S(1)} async-done(((bf16[8,192,192]{2,1,0:T(8,128)(2,1)}), bf16[8,192,192]{2,1,0:T(8,128)(2,1)S(1)}, u32[]{:S(2)}, u32[]{:S(2)}) %all-to-all-start.1) | async-done | bytes 589856 | tf_op jit(solution)/shard_map/all_to_all | solution.py:202
  504.4 5.4 gather_fusion.1
  515.0 44.6 %all-reduce.7 = (f32[2,192]{1,0:T(2,128)}, f32[768]{0:T(1024)S(1)}, f32[768]{0:T(1024)S(1)}, f32[768]{0:T(1024)S(1)}, f32[2,768]{1,0:T(2,128)}, /*index=5*/f32[7...) all-reduce(f32[2,192]{1,0:T(2,128)S(1)} %broadcast_multiply_fusion.10, ...), channel_id=1, replica_groups=mesh['dp'=8,'tensor'=4] {'dp'}, use_global_device_ids=true, to_apply=%region_19.20 | all-reduce | flops 6528 | bytes 52224 | tf_op jit(solution)/shard_map/psum | solution.py:197
  564.8 32.5 %reduce-scatter.15.cloned.1.call-done = f32[96,576]{1,0:T(8,128)} async-done(((f32[768,576]{1,0:T(8,128)}), f32[96,576]{1,0:T(8,128)}) %reduce-scatter.15.cloned.1.call-update) | async-done | bytes 221200
  599.2 170.4 %all-reduce.19.cloned.1.call-done = f32[2,768,768]{2,0,1:T(2,128)} async-done(((f32[2,768,768]{2,0,1:T(2,128)}), f32[2,768,768]{2,0,1:T(2,128)}) %all-reduce.19.cloned.1.call-update) | async-done | bytes 4718608
  772.7 69.6 %reduce-scatter.11.cloned.1.call-done = f32[768,96]{0,1:T(8,128)} async-done(((f32[768,768]{0,1:T(8,128)}), f32[768,96]{0,1:T(8,128)}) %reduce-scatter.11.cloned.1.call-update) | async-done | bytes 294928 | tf_op jit(solution)/shard_map/reduce_scatter | solution.py:178
  (240 shorter events, 129.7 us)
Async XLA Ops:
  7.2 190.1 %copy-start = (bf16[2,768,768]{2,1,0:T(8,128)(2,1)S(1)}, bf16[2,768,768]{2,1,0:T(8,128)(2,1)}, u32[]{:S(2)}) copy-start(bf16[2,768,768]{2,1,0:T(8,128)(2,1)} %param.26) | copy-start | bytes 7077892
  7.2 31.4 %copy-start.39 = (s32[1536]{0:T(1024)S(1)}, s32[1536]{0:T(1024)}, u32[]{:S(2)}) copy-start(s32[1536]{0:T(1024)} %param.18) | copy-start | bytes 18436
  7.2 31.5 %copy-start.40 = (s32[1,1536]{1,0:T(1,128)S(1)}, s32[1,1536]{1,0:T(1,128)}, u32[]{:S(2)}) copy-start(s32[1,1536]{1,0:T(1,128)} %param.19) | copy-start | bytes 18436
  7.2 31.5 %copy-start.43 = (bf16[2,192]{1,0:T(2,128)(2,1)S(1)}, bf16[2,192]{1,0:T(2,128)(2,1)}, u32[]{:S(2)}) copy-start(bf16[2,192]{1,0:T(2,128)(2,1)} %param.21) | copy-start | bytes 2308
  7.2 54.5 %all-gather.3.cloned.1.call-start = ((), (), s32[]{:S(2)}) async-start(), calls=%async_computation.8 | async-start | bytes 2949120 | tf_op jit(solution)/shard_map/all_gather | solution.py:67
  38.5 154.2 %all-reduce.13.cloned.1.call-start = ((), (), s32[]{:S(2)}) async-start(), calls=%async_computation.9 | async-start | bytes 9437184 | tf_op jit(solution)/shard_map/psum | solution.py:102
  38.8 27.3 %copy-start.29 = (s32[1536]{0:T(1024)}, s32[1536]{0:T(1024)S(1)}, u32[]{:S(2)}) copy-start(s32[1536]{0:T(1024)S(1)} %fusion.70) | copy-start | bytes 18436
  40.4 35.4 %copy-start.51 = (bf16[3,768,192]{1,2,0:T(8,128)(2,1)S(1)}, bf16[3,768,192]{1,2,0:T(8,128)(2,1)}, u32[]{:S(2)}) copy-start(bf16[3,768,192]{1,2,0:T(8,128)(2,1)} %param.20) | copy-start | bytes 2654212
  103.2 26.2 %all-to-all-start.2 = ((bf16[8,192,192]{1,2,0:T(8,128)(2,1)}), bf16[8,192,192]{1,2,0:T(8,128)(2,1)}, u32[]{:S(2)}, u32[]{:S(2)}) async-start(bf16[8,192,192]{1,2,0:T(8,128)(2,1)} %copy.133), calls=%async_computation.2 | async-start | bytes 1572864 | tf_op jit(solution)/shard_map/all_to_all | solution.py:64
  108.8 110.4 %all-gather.5.cloned.1.call-start = ((), (), s32[]{:S(2)}) async-start(), calls=%async_computation.11 | async-start | bytes 2949120 | tf_op jit(solution)/shard_map/all_gather | solution.py:68
  108.8 258.0 %copy-start.27 = (f32[768]{0:T(1024)}, f32[768]{0:T(1024)S(1)}, u32[]{:S(2)}) copy-start(f32[768]{0:T(1024)S(1)} %convert_element_type.142) | copy-start | bytes 9220
  108.9 168.2 %copy-start.33 = (f32[768]{0:T(1024)}, f32[768]{0:T(1024)S(1)}, u32[]{:S(2)}) copy-start(f32[768]{0:T(1024)S(1)} %convert_element_type.143) | copy-start | bytes 9220
  134.4 142.7 %all-reduce.15.cloned.1.call-start = ((), (), s32[]{:S(2)}) async-start(), calls=%async_computation.10 | async-start | bytes 4718592 | tf_op jit(solution)/shard_map/psum | solution.py:113
  201.6 11.5 %copy-start.8 = (f32[2,1536,768]{2,1,0:T(8,128)}, f32[2,1536,768]{2,1,0:T(8,128)S(1)}, u32[]{:S(2)}) copy-start(f32[2,1536,768]{2,1,0:T(8,128)S(1)} %add_bitcast_fusion) | copy-start | bytes 28311556
  201.6 13.0 %copy-start.50 = (bf16[768,768]{1,0:T(8,128)(2,1)S(1)}, bf16[768,768]{1,0:T(8,128)(2,1)}, u32[]{:S(2)}) copy-start(bf16[768,768]{1,0:T(8,128)(2,1)} %param.28) | copy-start | bytes 3538948
  218.1 142.2 %all-reduce.17.cloned.1.call-start = ((), (), s32[]{:S(2)}) async-start(), calls=%async_computation.12 | async-start | bytes 4718592 | tf_op jit(solution)/shard_map/psum | solution.py:131
  288.8 78.0 %copy-start.25 = (f32[1536]{0:T(1024)}, f32[1536]{0:T(1024)S(1)}, u32[]{:S(2)}) copy-start(f32[1536]{0:T(1024)S(1)} %negate_multiply_fusion.2) | copy-start | bytes 18436
  304.4 196.4 %reduce-scatter.13.cloned.1.call-start = ((), (), s32[]{:S(2)}) async-start(), calls=%async_computation.14 | async-start | bytes 2949120
  389.1 11.2 %copy-start.12 = (bf16[3,512,3,64]{1,0,3,2:T(4,128)(2,1)S(1)}, bf16[3,512,3,64]{1,0,3,2:T(4,128)(2,1)}, u32[]{:S(2)}) copy-start(bf16[3,512,3,64]{1,0,3,2:T(4,128)(2,1)} %copy-done.11) | copy-start | bytes 1769476
  407.6 13.8 %copy-start.13 = (bf16[1,1536,192]{1,2,0:T(8,128)(2,1)}, bf16[1,1536,192]{1,2,0:T(8,128)(2,1)S(1)}, u32[]{:S(2)}) copy-start(bf16[1,1536,192]{1,2,0:T(8,128)(2,1)S(1)} %stack.36) | copy-start | bytes 1769476
  421.4 141.7 %reduce-scatter.17.cloned.1.call-start = ((), (), s32[]{:S(2)}) async-start(), calls=%async_computation.16 | async-start | bytes 884736
  425.8 171.5 %reduce-scatter.15.cloned.1.call-start = ((), (), s32[]{:S(2)}) async-start(), calls=%async_computation.15 | async-start | bytes 2211840
  439.5 330.2 %all-reduce.19.cloned.1.call-start = ((), (), s32[]{:S(2)}) async-start(), calls=%async_computation.17 | async-start | bytes 9437184
  457.5 384.8 %reduce-scatter.11.cloned.1.call-start = ((), (), s32[]{:S(2)}) async-start(), calls=%async_computation.13 | async-start | bytes 2654208 | tf_op jit(solution)/shard_map/reduce_scatter | solution.py:178
  467.4 10.6 %copy-start.52 = (u32[32]{0:T(128)S(1)}, u32[32]{0:T(128)}, u32[]{:S(2)}) copy-start(u32[32]{0:T(128)} %constant.120) | copy-start | bytes 388
  467.4 11.9 %copy-start.35 = (f32[768]{0:T(1024)S(1)}, f32[768]{0:T(1024)}, u32[]{:S(2)}) copy-start(f32[768]{0:T(1024)} %get-tuple-element.115) | copy-start | bytes 9220
  472.8 27.0 %all-to-all-start.1 = ((bf16[8,192,192]{2,1,0:T(8,128)(2,1)}), bf16[8,192,192]{2,1,0:T(8,128)(2,1)S(1)}, u32[]{:S(2)}, u32[]{:S(2)}) async-start(bf16[8,192,192]{2,1,0:T(8,128)(2,1)} %bitcast.11), calls=%async_computation.1 | async-start | bytes 1572864 | tf_op jit(solution)/shard_map/all_to_all | solution.py:202
  504.4 10.6 %copy-start.32 = (f32[768]{0:T(1024)S(1)}, f32[768]{0:T(1024)}, u32[]{:S(2)}) copy-start(f32[768]{0:T(1024)} %get-tuple-element.90) | copy-start | bytes 9220
  504.4 10.6 %copy-start.36 = (f32[768]{0:T(1024)S(1)}, f32[768]{0:T(1024)}, u32[]{:S(2)}) copy-start(f32[768]{0:T(1024)} %get-tuple-element.86) | copy-start | bytes 9220
  504.4 10.6 %copy-start.37 = (f32[768]{0:T(1024)S(1)}, f32[768]{0:T(1024)}, u32[]{:S(2)}) copy-start(f32[768]{0:T(1024)} %get-tuple-element.87) | copy-start | bytes 9220
  504.4 337.8 %copy-start.1 = (bf16[2,768,768]{2,1,0:T(8,128)(2,1)S(1)}, bf16[2,768,768]{2,1,0:T(8,128)(2,1)}, u32[]{:S(2)}) copy-start(bf16[2,768,768]{2,1,0:T(8,128)(2,1)} %param.26) | copy-start | bytes 7077892
  509.8 261.8 %all-to-all-start.3 = ((bf16[8,192,192]{2,1,0:T(8,128)(2,1)}), bf16[8,192,192]{2,1,0:T(8,128)(2,1)S(1)}, u32[]{:S(2)}, u32[]{:S(2)}) async-start(bf16[8,192,192]{2,1,0:T(8,128)(2,1)} %bitcast.200), calls=%async_computation.3 | async-start | bytes 1572864 | tf_op jit(solution)/shard_map/all_to_all | solution.py:203
  (39 other events, 215.1 us)
Sparse Core Ops, SparseCore 0:
  38.7 23.0 all-gather.2
  98.7 94.0 all-reduce.12
  194.9 24.1 all-gather.4
  221.4 55.6 all-reduce.14
  304.5 55.7 all-reduce.16
  421.5 32.8 reduce-scatter.12
  457.7 66.9 reduce-scatter.16
  528.2 69.0 reduce-scatter.14
  600.9 168.6 all-reduce.18
  773.5 68.6 reduce-scatter.10
where the time goes:
time: 856 us; the launch traced here: 850 us
  waiting for transfers between devices  487 us (57%)
  local copies, waits for them, and re-layouts  110 us (13%)
  matrix products  82.2 us (10%)
  blocking collectives  71.9 us (8%)
  other arithmetic  66.4 us (8%)
  between operations  16.3 us (2%)
  starting transfers between devices  15.5 us (2%)
    unnamed x14, waiting for transfers between devices  203 us
    reduce_scatter x1, waiting for transfers between devices, on_device(): lax.psum_scatter(g_down * grad_scale, 'dp', scatter_dimension=1, tiled=True)  69.6 us
    psum x1, waiting for transfers between devices, on_device(): attended = lax.psum(attn_part, 'tensor')  58.1 us
    psum x1, waiting for transfers between devices, on_device(): lax.psum(d_normed_part.astype(jnp.bfloat16), 'tensor').astype(jnp.float32)  55 us
    psum x1, blocking collectives, on_device(): lax.psum((g_qv_bias * grad_scale, g_up_bias * grad_scale), 'dp')  44.6 us
    psum x1, waiting for transfers between devices, on_device(): lax.psum(ffn_part.astype(jnp.bfloat16), 'tensor').astype(jnp.float32)  43.6 us
    unnamed x135, local copies, waits for them, and re-layouts  31.6 us
    all_to_all x1, blocking collectives, on_device(): lax.all_to_all(tokens, 'dp', split_axis=0, concat_axis=0, tiled=True)  27.3 us
  transfers between devices with their start and end apart: 13, of which 10 were waited for; matrix products, arithmetic and copies ran while one was open for 14% of the time, Pallas kernels for 0%

commit v1 on v0

v1 whole, which is shorter than its diff:
```python
import jax
import jax.numpy as jnp
from jax import lax
from jax.sharding import PartitionSpec as P

HEADS = 12
HEAD_DIM = 64
BLOCK = 512
BF = jnp.bfloat16
F32 = jnp.float32


def dot(a, b, dims):
    return lax.dot_general(a, b, (dims, ((), ())), preferred_element_type=F32)


def alibi_terms(part_index, local_heads, block_rows):
    heads_idx = (part_index * local_heads + jnp.arange(local_heads)).astype(F32)
    slopes = 2.0 ** (-8.0 * (heads_idx + 1.0) / HEADS)
    position = jnp.arange(block_rows).astype(F32)
    distance = jnp.abs(position[:, None] - position[None, :])
    return -slopes[:, None, None] * distance[None]


def block_scores(queries, key_rows, alibi_bias, same_seq, score_scale):
    raw_scores = jnp.einsum("bqhe,bkhe->bhqk", queries, key_rows, preferred_element_type=F32)
    scored = raw_scores * score_scale + alibi_bias[None]
    return jnp.where(same_seq[:, None], scored, -1e30)


def softmax_rows(scored):
    row_max = jnp.max(scored, axis=-1, keepdims=True)
    exponent = jnp.exp(scored - row_max)
    denominator = jnp.sum(exponent, axis=-1, keepdims=True)
    return (exponent / denominator, row_max + jnp.log(denominator))


def gather_columns(rows):
    return lax.all_gather(rows, "tensor", axis=1, tiled=True)


def scatter_columns(rows):
    return lax.psum_scatter(rows, "tensor", scatter_dimension=1, tiled=True)


def merge_stats(values, weighted, columns):
    width = values.shape[1]
    own_mean = jnp.mean(values, axis=1)
    offset = values - own_mean[:, None]
    parts = jnp.stack(
        [own_mean, jnp.sum(offset * offset, axis=1), jnp.sum(weighted, axis=1), jnp.sum(weighted * offset, axis=1)]
    )
    shares = lax.all_gather(parts, "tensor", axis=0)
    mean = jnp.mean(shares[:, 0], axis=0)
    gap = shares[:, 0] - mean
    spread = jnp.sum(shares[:, 1] + width * gap * gap, axis=0) / columns
    rs = lax.rsqrt(spread + 1e-05)
    e_mean = jnp.sum(shares[:, 2], axis=0) / columns
    en_mean = rs * jnp.sum(shares[:, 3] + gap * shares[:, 2], axis=0) / columns
    return mean[:, None], rs[:, None], e_mean[:, None], en_mean[:, None]


def on_device(
    tokens,
    cotangent,
    seq_start,
    row_place,
    qkv_weight,
    qv_bias,
    out_weight,
    out_bias,
    first_gain,
    first_shift,
    up_weight,
    up_bias,
    down_weight,
    down_bias,
    second_gain,
    second_shift,
):
    row_count = tokens.shape[0]
    width = tokens.shape[1]
    columns = qkv_weight.shape[1]
    local_heads = qkv_weight.shape[2] // HEAD_DIM
    blocks = row_count // BLOCK
    part_index = lax.axis_index("tensor")
    score_scale = HEAD_DIM ** (-0.5)
    grad_scale = (row_count * lax.axis_size("dp")) ** (-0.5)

    def own(vector):
        return lax.dynamic_slice_in_dim(vector.astype(F32), part_index * width, width, 0)

    arr_tokens = lax.all_to_all(tokens, "dp", split_axis=0, concat_axis=0, tiled=True)
    arr_cot = lax.all_to_all(cotangent, "dp", split_axis=0, concat_axis=0, tiled=True)
    slot_index = row_place[0]
    row_ids = lax.broadcasted_iota(jnp.int32, (row_count, row_count), 0)
    placing = (row_ids == slot_index[None, :]).astype(BF)
    in_cols = dot(placing, arr_tokens, ((1,), (0,))).astype(BF)
    cot_cols = dot(placing, arr_cot, ((1,), (0,))).astype(BF)
    packed_in = gather_columns(in_cols)
    full_out = lax.all_gather(out_weight, "tensor", axis=0, tiled=True)

    alibi_bias = alibi_terms(part_index, local_heads, BLOCK)
    block_starts = seq_start.reshape(blocks, BLOCK)
    same_seq = block_starts[:, :, None] == block_starts[:, None, :]
    bias_rows = jnp.stack([qv_bias[0], jnp.zeros_like(qv_bias[0]), qv_bias[1]]).astype(F32)
    projected = jnp.einsum("td,kde->kte", packed_in, qkv_weight, preferred_element_type=F32)
    qkv_rows = (projected + bias_rows[:, None, :]).astype(BF)
    split_heads = qkv_rows.reshape(3, blocks, BLOCK, local_heads, HEAD_DIM)
    queries = split_heads[0]
    key_rows = split_heads[1]
    value_rows = split_heads[2]
    attn_probs, log_total = softmax_rows(block_scores(queries, key_rows, alibi_bias, same_seq, score_scale))
    context = jnp.einsum("bhqk,bkhe->bqhe", attn_probs.astype(BF), value_rows, preferred_element_type=F32)
    context = context.reshape(row_count, local_heads * HEAD_DIM).astype(BF)

    wide_context = gather_columns(context)
    attended = dot(wide_context, full_out, ((1,), (0,)))
    hidden = packed_in.astype(F32) + (attended + out_bias.astype(F32))
    center = hidden - jnp.mean(hidden, axis=1, keepdims=True)
    first_rs = lax.rsqrt(jnp.mean(center * center, axis=1, keepdims=True) + 1e-05)
    normed = center * first_rs * first_gain.astype(F32) + first_shift.astype(F32)
    normed_low = normed.astype(BF)
    first_unit = lax.dynamic_slice_in_dim(center * first_rs, part_index * width, width, 1)
    normed_cols = first_unit * own(first_gain) + own(first_shift)

    lifted = jnp.einsum("td,kdf->ktf", normed_low, up_weight, preferred_element_type=F32)
    lifted = lifted + up_bias.astype(F32)[:, None, :]
    half_erf = 0.5 * (1.0 + lax.erf(lifted[0] * (0.5**0.5)))
    gelu_gate = lifted[0] * half_erf
    gated_low = (gelu_gate * lifted[1]).astype(BF)
    ffn_part = dot(gated_low, down_weight, ((1,), (0,)))
    ffn_cols = scatter_columns(ffn_part.astype(BF)).astype(F32)
    mixed_cols = normed_cols + (ffn_cols + own(down_bias))
    cot_wide = cot_cols.astype(F32)
    weighted = cot_wide * own(second_gain)
    mean, rs, e_mean, en_mean = merge_stats(mixed_cols, weighted, columns)
    second_unit = (mixed_cols - mean) * rs
    result_cols = second_unit * own(second_gain) + own(second_shift)
    d_mixed_cols = rs * (weighted - e_mean - second_unit * en_mean)
    d_second_gain = jnp.sum(cot_wide * second_unit, axis=0)
    d_second_shift = jnp.sum(cot_wide, axis=0)
    g_down_bias = jnp.sum(d_mixed_cols, axis=0)

    def unpacked(rows):
        placed = dot(placing, rows, ((0,), (0,))).astype(BF)
        return lax.all_to_all(placed, "dp", split_axis=0, concat_axis=0, tiled=True)

    layer_out = unpacked(result_cols.astype(BF))

    d_mixed_low = gather_columns(d_mixed_cols.astype(BF))
    g_down = dot(d_mixed_low, gated_low, ((0,), (0,)))
    d_gated = dot(d_mixed_low, down_weight, ((1,), (1,)))
    gelu_slope = half_erf + lifted[0] * jnp.exp(-0.5 * lifted[0] * lifted[0]) * ((2.0 * jnp.pi) ** (-0.5))
    d_gate = (d_gated * lifted[1] * gelu_slope).astype(BF)
    d_value = (d_gated * gelu_gate).astype(BF)
    g_gate = dot(normed_low, d_gate, ((0,), (0,)))
    g_value = dot(normed_low, d_value, ((0,), (0,)))
    g_up_bias = jnp.stack([jnp.sum(d_gate, axis=0, dtype=F32), jnp.sum(d_value, axis=0, dtype=F32)])
    d_normed_part = dot(d_gate, up_weight[0], ((1,), (1,))) + dot(d_value, up_weight[1], ((1,), (1,)))
    d_normed_cols = d_mixed_cols + scatter_columns(d_normed_part.astype(BF)).astype(F32)

    first_weighted = d_normed_cols * own(first_gain)
    shares = lax.all_gather(
        jnp.stack([jnp.sum(first_weighted, axis=1), jnp.sum(first_weighted * first_unit, axis=1)]), "tensor", axis=0
    )
    totals = jnp.sum(shares, axis=0) / columns
    own_rs = first_rs
    d_hidden_cols = own_rs * (first_weighted - totals[0][:, None] - first_unit * totals[1][:, None])
    d_first_gain = jnp.sum(d_normed_cols * first_unit, axis=0)
    d_first_shift = jnp.sum(d_normed_cols, axis=0)
    g_out_bias = jnp.sum(d_hidden_cols, axis=0)
    d_hidden_low = gather_columns(d_hidden_cols.astype(BF))
    g_out = dot(d_hidden_low, context, ((0,), (0,)))
    d_context = dot(d_hidden_low, out_weight, ((1,), (1,)))
    d_context = d_context.astype(BF).reshape(blocks, BLOCK, local_heads, HEAD_DIM)
    probs_back = jnp.exp(block_scores(queries, key_rows, alibi_bias, same_seq, score_scale) - log_total)
    d_probs = jnp.einsum("bqhe,bkhe->bhqk", d_context, value_rows, preferred_element_type=F32)
    g_values = jnp.einsum("bhqk,bqhe->bkhe", probs_back.astype(BF), d_context, preferred_element_type=F32)
    center_term = jnp.sum(probs_back * d_probs, axis=-1, keepdims=True)
    d_scores = (probs_back * (d_probs - center_term)).astype(BF)
    g_queries = jnp.einsum("bhqk,bkhe->bqhe", d_scores, key_rows, preferred_element_type=F32) * score_scale
    g_keys = jnp.einsum("bhqk,bqhe->bkhe", d_scores, queries, preferred_element_type=F32) * score_scale
    d_query, d_key, d_value_rows = (
        part.astype(BF).reshape(row_count, local_heads * HEAD_DIM) for part in (g_queries, g_keys, g_values)
    )
    d_qkv = jnp.concatenate([d_query, d_key, d_value_rows], axis=1)
    side = qkv_weight.transpose(1, 0, 2).reshape(columns, 3 * width)
    g_qkv = dot(packed_in, d_qkv, ((0,), (0,)))
    g_qv_bias = jnp.stack([jnp.sum(d_query, axis=0, dtype=F32), jnp.sum(d_value_rows, axis=0, dtype=F32)])
    d_input_part = dot(d_qkv, side, ((1,), (1,)))
    grad_cols = d_hidden_cols + scatter_columns(d_input_part.astype(BF)).astype(F32)
    input_grad = unpacked(grad_cols.astype(BF))

    def over_groups(grad):
        return lax.psum_scatter((grad * grad_scale).astype(BF), "dp", scatter_dimension=0, tiled=True).astype(F32)

    down_grad = over_groups(g_down).T
    up_grad = jnp.stack([over_groups(g_gate), over_groups(g_value)])
    late = over_groups(jnp.concatenate([g_qkv, g_out], axis=1))
    qkv_grad = late[:, : 3 * width].reshape(-1, 3, width).transpose(1, 0, 2)
    out_grad = late[:, 3 * width :].T

    split_sums = jnp.stack([g_out_bias, d_first_gain, d_first_shift, g_down_bias, d_second_gain, d_second_shift])
    flat = jnp.concatenate([split_sums.reshape(-1), g_qv_bias.reshape(-1), g_up_bias.reshape(-1)]) * grad_scale
    flat = jnp.sum(lax.all_gather(flat, "dp", axis=0), axis=0)
    cut = 6 * width
    wide_sums = lax.all_gather(flat[:cut].reshape(6, width), "tensor", axis=1, tiled=True)
    rows_here = columns // lax.axis_size("dp")
    sums_here = lax.dynamic_slice_in_dim(wide_sums, lax.axis_index("dp") * rows_here, rows_here, 1)
    qv_bias_grad = flat[cut : cut + 2 * width].reshape(2, width)
    up_bias_grad = flat[cut + 2 * width :].reshape(2, -1)
    return (
        layer_out,
        input_grad,
        qkv_grad,
        qv_bias_grad,
        out_grad,
        sums_here[0],
        sums_here[1],
        sums_here[2],
        up_grad,
        up_bias_grad,
        down_grad,
        sums_here[3],
        sums_here[4],
        sums_here[5],
    )


def solution(mesh):
    return jax.shard_map(
        on_device,
        mesh=mesh,
        in_specs=(
            P("dp", "tensor"),
            P("dp", "tensor"),
            P("dp"),
            P("dp", None),
            P(None, None, "tensor"),
            P(None, "tensor"),
            P("tensor", None),
            P(),
            P(),
            P(),
            P(None, None, "tensor"),
            P(None, "tensor"),
            P("tensor", None),
            P(),
            P(),
            P(),
        ),
        out_specs=(
            P("dp", "tensor"),
            P("dp", "tensor"),
            P(None, "dp", "tensor"),
            P(None, "tensor"),
            P("tensor", "dp"),
            P("dp"),
            P("dp"),
            P("dp"),
            P(None, "dp", "tensor"),
            P(None, "tensor"),
            P("tensor", "dp"),
            P("dp"),
            P("dp"),
            P("dp"),
        ),
        check_vma=False,
    )
```

time: 856 us -> 615 us (0.72)
  waiting for transfers between devices: 487 us -> 334 us
  local copies, waits for them, and re-layouts: 110 us -> 52.3 us
  other arithmetic: 66.4 us -> 30.2 us
  starting transfers between devices: 15.5 us -> 25.7 us
    psum x3 -> x0, waiting for transfers between devices: 157 us -> none  [the longest x1 58.1 us: on_device(): attended = lax.psum(attn_part, 'tensor')]
    unnamed x14 -> x16, waiting for transfers between devices: 203 us -> 137 us
    all_gather x0 -> x4, blocking collectives: none -> 64.3 us  [the longest x1 48.6 us: on_device(): flat = jnp.sum(lax.all_gather(flat, 'dp', axis=0), axis=0)]
    all_gather x2 -> x5, waiting for transfers between devices: 20.2 us -> 73 us  [the longest x4 73 us: gather_columns(): return lax.all_gather(rows, 'tensor', axis=1, tiled=True)]
    psum x1 -> x0, blocking collectives: 44.6 us -> none  [on_device(): lax.psum((g_qv_bias * grad_scale, g_up_bias * grad_scale), 'dp')]
    all_to_all x1 -> x0, blocking collectives: 27.3 us -> none  [on_device(): lax.all_to_all(tokens, 'dp', split_axis=0, concat_axis=0, tiled=True)]
    reduce_sum x10 -> x8, other arithmetic: 33.3 us -> 6.37 us  [the longest x1 1.95 us: on_device(): d_first_gain = jnp.sum(d_normed_cols * first_unit, axis=0)]
    all_to_all x2 -> x3, waiting for transfers between devices: 17.3 us -> 38.5 us  [the longest x1 20.1 us: on_device(): lax.all_to_all(tokens, 'dp', split_axis=0, concat_axis=0, tiled=True)]
  transfers between devices with their start and end apart: 13 -> 16, of which waited for: 10 -> 13; matrix products, arithmetic and copies ran while one was open for 14% -> 17% of each run, Pallas kernels for 0% -> 0%
where the time goes in v1:
time: 615 us; the launch traced here: 611 us
  waiting for transfers between devices  334 us (54%)
  matrix products  88.8 us (14%)
  blocking collectives  64.3 us (10%)
  local copies, waits for them, and re-layouts  52.3 us (9%)
  other arithmetic  30.2 us (5%)
  starting transfers between devices  25.7 us (4%)
  between operations  15.5 us (3%)
    unnamed x16, waiting for transfers between devices  137 us
    all_gather x4, waiting for transfers between devices, gather_columns(): return lax.all_gather(rows, 'tensor', axis=1, tiled=True)  73 us
    reduce_scatter x3, waiting for transfers between devices, scatter_columns(): return lax.psum_scatter(rows, 'tensor', scatter_dimension=1, tiled=True)  65.7 us
    dot_general x16, matrix products, dot(): return lax.dot_general(a, b, (dims, ((), ())), preferred_element_type=F32)  56.8 us
    all_gather x1, blocking collectives, on_device(): flat = jnp.sum(lax.all_gather(flat, 'dp', axis=0), axis=0)  48.6 us
    unnamed x88, local copies, waits for them, and re-layouts  24.2 us
    all_to_all x1, waiting for transfers between devices, on_device(): lax.all_to_all(tokens, 'dp', split_axis=0, concat_axis=0, tiled=True)  20.1 us
    all_to_all x1, waiting for transfers between devices, on_device(): lax.all_to_all(cotangent, 'dp', split_axis=0, concat_axis=0, tiled=True)  19.8 us
  transfers between devices with their start and end apart: 16, of which 13 were waited for; matrix products, arithmetic and copies ran while one was open for 17% of the time, Pallas kernels for 0%

profile of v1, /device:TPU:0, one launch (start us, length us, event | category | flops | bytes accessed | tf_op | source)
XLA Modules:
  0.0 610.8 jit_solution(10734552117555478064)
XLA Ops:
  10.1 7.3 %all-to-all-start = ((bf16[8,192,192]{1,2,0:T(8,128)(2,1)}), bf16[8,192,192]{1,2,0:T(8,128)(2,1)S(1)}, u32[]{:S(2)}, u32[]{:S(2)}) async-start(bf16[8,192,192]{1,2,0:T(8,128)(2,1)} %copy.106), calls=%async_computation | async-start | bytes 1572864 | tf_op jit(solution)/shard_map/all_to_all | solution.py:93
  17.5 20.1 %all-to-all-done = bf16[8,192,192]{1,2,0:T(8,128)(2,1)S(1)} async-done(((bf16[8,192,192]{1,2,0:T(8,128)(2,1)}), bf16[8,192,192]{1,2,0:T(8,128)(2,1)S(1)}, u32[]{:S(2)}, u32[]{:S(2)}) %all-to-all-start) | async-done | bytes 589856 | tf_op jit(solution)/shard_map/all_to_all | solution.py:93
  46.5 18.3 %all-gather.12.cloned.1.call-done = bf16[1536,768]{0,1:T(8,128)(2,1)} async-done(((bf16[1536,192]{0,1:T(8,128)(2,1)}), bf16[1536,768]{0,1:T(8,128)(2,1)}) %all-gather.12.cloned.1.call-update) | async-done | bytes 2359312 | tf_op jit(solution)/shard_map/all_gather | solution.py:39
  72.4 5.1 fusion.72
  85.0 25.1 %all-gather.14.cloned.1.call-done = bf16[1536,768]{0,1:T(8,128)(2,1)} async-done(((bf16[1536,192]{0,1:T(8,128)(2,1)}), bf16[1536,768]{0,1:T(8,128)(2,1)}) %all-gather.14.cloned.1.call-update) | async-done | bytes 2359312 | tf_op jit(solution)/shard_map/all_gather | solution.py:39
  110.1 5.1 fusion.73
  118.8 3.9 add_bitcast_fusion
  135.5 5.5 all-to-all-start.1
  141.8 19.8 %all-to-all-done.1 = bf16[8,192,192]{1,2,0:T(8,128)(2,1)S(1)} async-done(((bf16[8,192,192]{1,2,0:T(8,128)(2,1)}), bf16[8,192,192]{1,2,0:T(8,128)(2,1)S(1)}, u32[]{:S(2)}, u32[]{:S(2)}) %all-to-all-start.1) | async-done | bytes 589856 | tf_op jit(solution)/shard_map/all_to_all | solution.py:94
  170.1 5.3 all-gather.2
  177.2 24.2 %all-gather.18.cloned.1.call-done = bf16[1536,768]{0,1:T(8,128)(2,1)} async-done(((bf16[1536,192]{0,1:T(8,128)(2,1)}), bf16[1536,768]{0,1:T(8,128)(2,1)}) %all-gather.18.cloned.1.call-update) | async-done | bytes 2359312 | tf_op jit(solution)/shard_map/all_gather | solution.py:39
  201.3 7.6 %convert_reduce_fusion = (f32[768]{0:T(1024)S(1)}, bf16[1536,768]{1,0:T(8,128)(2,1)S(1)}, f32[768]{0:T(1024)S(1)}, bf16[1536,768]{1,0:T(8,128)(2,1)S(1)}) fusion(f32[2,1536,768]{2,1,0:T(8,128)} %copy-done.4, bf16[1536,768]{0,1:T(8,128)(2,1)} %all-gather.18.cloned.1.call-done, bf16[768,768]{1,0:T(8,128)(2,1)S(1)} %copy-done), kind=kOutput, calls=%fused_computation.24 | convolution fusion | flops 1833171456 | bytes 17700864 | tf_op jit(solution)/shard_map/dot_general | solution.py:14
  214.8 32.9 %reduce-scatter.18.cloned.1.call-done = bf16[1536,192]{0,1:T(8,128)(2,1)} async-done(((bf16[1536,768]{0,1:T(8,128)(2,1)}), bf16[1536,192]{0,1:T(8,128)(2,1)}) %reduce-scatter.18.cloned.1.call-update) | async-done | bytes 589840 | tf_op jit(solution)/shard_map/reduce_scatter | solution.py:43
  249.7 5.2 all-gather.3
  258.0 4.4 multiply_convert_fusion.3
  264.0 5.0 multiply_convert_fusion.5
  270.5 4.4 multiply_convert_fusion.4
  276.5 5.5 all-gather.20.cloned.1.call-done
  284.8 5.4 convert_reduce_fusion.2
  290.2 7.4 %multiply_reduce_fusion = (f32[3,3,512]{2,1,0:T(4,128)S(1)}, f32[3,3,512,512]{2,3,1,0:T(8,128)}) fusion(f32[3,3,512,512]{2,3,1,0:T(8,128)} %copy-done.2, f32[3,3,512]{2,1,0:T(4,128)S(1)} %log_add_fusion, bf16[3,512,3,64]{1,0,3,2:T(4,128)(2,1)S(1)} %copy-done.12, bf16[3,512,3,64]{1,0,3,2:T(4,128)(2,1)S(1)} %reshape.281), kind=kOutput, calls=%fused_computation.1 | convolution fusion | flops 309063168 | bytes 20090880 | tf_op jit(solution)/shard_map/bqhe,bkhe->bhqk/dot_general | solution.py:178
  298.3 11.2 %multiply_convert_fusion = bf16[3,3,512,512]{2,3,1,0:T(8,128)(2,1)} fusion(f32[3,3,512,512]{2,3,1,0:T(8,128)} %get-tuple-element.123, f32[3,3,512,512]{2,3,1,0:T(8,128)} %copy-done.2, f32[3,3,512]{2,1,0:T(4,128)S(1)} %get-tuple-element.122, f32[3,3,512]{2,1,0:T(4,128)S(1)} %log_add_fusion), kind=kLoop, calls=%fused_computation | loop fusion | flops 9437184 | bytes 23629824 | tf_op jit(solution)/shard_map/convert_element_type | solution.py:181
  309.6 4.0 fusion.39
  326.2 5.6 all-to-all-start.2
  332.2 3.9 fusion.74
  338.8 18.4 %all-to-all-done.2 = bf16[8,192,192]{1,2,0:T(8,128)(2,1)S(1)} async-done(((bf16[8,192,192]{1,2,0:T(8,128)(2,1)}), bf16[8,192,192]{1,2,0:T(8,128)(2,1)S(1)}, u32[]{:S(2)}, u32[]{:S(2)}) %all-to-all-start.2) | async-done | bytes 589856 | tf_op jit(solution)/shard_map/all_to_all | solution.py:147
  361.2 62.1 %reduce-scatter.24.cloned.1.call-done = bf16[96,768]{1,0:T(8,128)(2,1)} async-done(((bf16[768,768]{1,0:T(8,128)(2,1)}), bf16[96,768]{1,0:T(8,128)(2,1)}) %reduce-scatter.24.cloned.1.call-update) | async-done | bytes 147472
  424.3 66.0 %reduce-scatter.26.cloned.1.call-done = bf16[96,768]{1,0:T(8,128)(2,1)} async-done(((bf16[768,768]{1,0:T(8,128)(2,1)}), bf16[96,768]{1,0:T(8,128)(2,1)}) %reduce-scatter.26.cloned.1.call-update) | async-done | bytes 147472
  492.9 31.8 %reduce-scatter.20.cloned.1.call-done = bf16[1536,192]{0,1:T(8,128)(2,1)} async-done(((bf16[1536,768]{0,1:T(8,128)(2,1)}), bf16[1536,192]{0,1:T(8,128)(2,1)}) %reduce-scatter.20.cloned.1.call-update) | async-done | bytes 589840 | tf_op jit(solution)/shard_map/reduce_scatter | solution.py:43
  529.4 5.5 all-to-all-start.3
  535.0 48.6 %all-gather.4 = f32[8,1,3072]{2,1,0:T(1,128)S(1)} all-gather(f32[1,1,3072]{2,1,0:T(1,128)S(1)} %fusion.64), channel_id=1, replica_groups=mesh['dp'=8,'tensor'=4] {'dp'}, dimensions={0}, use_global_device_ids=true | all-gather | bytes 110592 | tf_op jit(solution)/shard_map/all_gather | solution.py:206
  585.1 5.2 all-gather.5
  590.9 8.1 %reduce-scatter.22.cloned.1.call-done = bf16[96,768]{1,0:T(8,128)(2,1)} async-done(((bf16[768,768]{1,0:T(8,128)(2,1)}), bf16[96,768]{1,0:T(8,128)(2,1)}) %reduce-scatter.22.cloned.1.call-update) | async-done | bytes 147472
  (230 shorter events, 107.2 us)
Async XLA Ops:
  7.2 121.9 %copy-start = (bf16[768,768]{1,0:T(8,128)(2,1)S(1)}, bf16[768,768]{1,0:T(8,128)(2,1)}, u32[]{:S(2)}) copy-start(bf16[768,768]{1,0:T(8,128)(2,1)} %param.28) | copy-start | bytes 3538948
  7.2 10.2 %copy-start.20 = (s32[1,1536]{1,0:T(1,128)S(1)}, s32[1,1536]{1,0:T(1,128)}, u32[]{:S(2)}) copy-start(s32[1,1536]{1,0:T(1,128)} %param.19) | copy-start | bytes 18436
  10.1 27.5 %all-to-all-start = ((bf16[8,192,192]{1,2,0:T(8,128)(2,1)}), bf16[8,192,192]{1,2,0:T(8,128)(2,1)S(1)}, u32[]{:S(2)}, u32[]{:S(2)}) async-start(bf16[8,192,192]{1,2,0:T(8,128)(2,1)} %copy.106), calls=%async_computation | async-start | bytes 1572864 | tf_op jit(solution)/shard_map/all_to_all | solution.py:93
  17.4 47.5 %all-gather.12.cloned.1.call-start = ((), (), s32[]{:S(2)}) async-start(), calls=%async_computation.11 | async-start | bytes 2949120 | tf_op jit(solution)/shard_map/all_gather | solution.py:39
  38.7 4.0 copy-start.19
  41.6 43.4 %all-gather.16.cloned.1.call-start = ((), (), s32[]{:S(2)}) async-start(), calls=%async_computation.13 | async-start | bytes 1474560 | tf_op jit(solution)/shard_map/all_gather | solution.py:101
  42.4 67.7 %all-gather.14.cloned.1.call-start = ((), (), s32[]{:S(2)}) async-start(), calls=%async_computation.12 | async-start | bytes 2949120 | tf_op jit(solution)/shard_map/all_gather | solution.py:39
  44.2 20.6 %copy-start.31 = (bf16[3,768,192]{1,2,0:T(8,128)(2,1)S(1)}, bf16[3,768,192]{1,2,0:T(8,128)(2,1)}, u32[]{:S(2)}) copy-start(bf16[3,768,192]{1,2,0:T(8,128)(2,1)} %param.20) | copy-start | bytes 2654212
  70.8 6.7 %copy-start.5 = (bf16[3,512,3,64]{1,0,3,2:T(4,128)(2,1)}, bf16[3,512,3,64]{1,0,3,2:T(4,128)(2,1)S(1)}, u32[]{:S(2)}) copy-start(bf16[3,512,3,64]{1,0,3,2:T(4,128)(2,1)S(1)} %squeeze.60) | copy-start | bytes 1769476
  84.6 81.0 %reduce-scatter.16.cloned.1.call-start = ((), (), s32[]{:S(2)}) async-start(), calls=%async_computation.14 | async-start | bytes 2949120 | tf_op jit(solution)/shard_map/reduce_scatter | solution.py:43
  132.7 8.9 %copy-start.26 = (bf16[768]{0:T(1024)(128)(2,1)S(1)}, bf16[768]{0:T(1024)(128)(2,1)}, u32[]{:S(2)}) copy-start(bf16[768]{0:T(1024)(128)(2,1)} %param.30) | copy-start | bytes 4612
  132.7 9.0 %copy-start.27 = (bf16[768]{0:T(1024)(128)(2,1)S(1)}, bf16[768]{0:T(1024)(128)(2,1)}, u32[]{:S(2)}) copy-start(bf16[768]{0:T(1024)(128)(2,1)} %param.29) | copy-start | bytes 4612
  135.5 26.1 %all-to-all-start.1 = ((bf16[8,192,192]{1,2,0:T(8,128)(2,1)}), bf16[8,192,192]{1,2,0:T(8,128)(2,1)S(1)}, u32[]{:S(2)}, u32[]{:S(2)}) async-start(bf16[8,192,192]{1,2,0:T(8,128)(2,1)} %copy.114), calls=%async_computation.2 | async-start | bytes 1572864 | tf_op jit(solution)/shard_map/all_to_all | solution.py:94
  141.0 60.3 %all-gather.18.cloned.1.call-start = ((), (), s32[]{:S(2)}) async-start(), calls=%async_computation.15 | async-start | bytes 2949120 | tf_op jit(solution)/shard_map/all_gather | solution.py:39
  167.4 8.1 %copy-start.7 = (f32[1536,192]{0,1:T(8,128)}, f32[1536,192]{0,1:T(8,128)S(1)}, u32[]{:S(2)}) copy-start(f32[1536,192]{0,1:T(8,128)S(1)} %get-tuple-element.94) | copy-start | bytes 3538948
  177.1 70.5 %reduce-scatter.18.cloned.1.call-start = ((), (), s32[]{:S(2)}) async-start(), calls=%async_computation.16 | async-start | bytes 2949120 | tf_op jit(solution)/shard_map/reduce_scatter | solution.py:43
  201.3 7.6 %copy-start.30 = (bf16[2,768,768]{2,1,0:T(8,128)(2,1)S(1)}, bf16[2,768,768]{2,1,0:T(8,128)(2,1)}, u32[]{:S(2)}) copy-start(bf16[2,768,768]{2,1,0:T(8,128)(2,1)} %param.26) | copy-start | bytes 7077892
  214.7 67.3 %all-gather.20.cloned.1.call-start = ((), (), s32[]{:S(2)}) async-start(), calls=%async_computation.17 | async-start | bytes 2949120 | tf_op jit(solution)/shard_map/all_gather | solution.py:39
  256.8 5.6 copy-start.9
  257.8 101.4 %reduce-scatter.28.cloned.1.call-start = ((), (), s32[]{:S(2)}) async-start(), calls=%async_computation.22 | async-start | bytes 1327104
  264.0 159.3 %reduce-scatter.24.cloned.1.call-start = ((), (), s32[]{:S(2)}) async-start(), calls=%async_computation.20 | async-start | bytes 1327104
  270.4 219.9 %reduce-scatter.26.cloned.1.call-start = ((), (), s32[]{:S(2)}) async-start(), calls=%async_computation.21 | async-start | bytes 1327104
  275.0 7.0 %copy-start.17 = (bf16[192,768]{1,0:T(8,128)(2,1)S(1)}, bf16[192,768]{1,0:T(8,128)(2,1)}, u32[]{:S(2)}) copy-start(bf16[192,768]{1,0:T(8,128)(2,1)} %param.22) | copy-start | bytes 884740
  276.5 248.2 %reduce-scatter.20.cloned.1.call-start = ((), (), s32[]{:S(2)}) async-start(), calls=%async_computation.18 | async-start | bytes 2949120 | tf_op jit(solution)/shard_map/reduce_scatter | solution.py:43
  284.7 5.4 copy-start.12
  309.6 4.7 copy-start.3
  326.2 31.0 %all-to-all-start.2 = ((bf16[8,192,192]{1,2,0:T(8,128)(2,1)}), bf16[8,192,192]{1,2,0:T(8,128)(2,1)S(1)}, u32[]{:S(2)}, u32[]{:S(2)}) async-start(bf16[8,192,192]{1,2,0:T(8,128)(2,1)} %copy.118), calls=%async_computation.3 | async-start | bytes 1572864 | tf_op jit(solution)/shard_map/all_to_all | solution.py:147
  331.9 4.2 copy-start.15
  331.9 267.1 %reduce-scatter.22.cloned.1.call-start = ((), (), s32[]{:S(2)}) async-start(), calls=%async_computation.19 | async-start | bytes 1327104
  360.3 164.5 %copy-start.10 = (f32[1536,192]{0,1:T(8,128)S(1)}, f32[1536,192]{0,1:T(8,128)}, u32[]{:S(2)}) copy-start(f32[1536,192]{0,1:T(8,128)} %copy-done.9) | copy-start | bytes 3538948
  529.4 72.4 %all-to-all-start.3 = ((bf16[8,192,192]{1,2,0:T(8,128)(2,1)}), bf16[8,192,192]{1,2,0:T(8,128)(2,1)S(1)}, u32[]{:S(2)}, u32[]{:S(2)}) async-start(bf16[8,192,192]{1,2,0:T(8,128)(2,1)} %copy.132), calls=%async_computation.6 | async-start | bytes 1572864 | tf_op jit(solution)/shard_map/all_to_all | solution.py:147
  599.0 4.7 copy-start.1
  (19 other events, 44.6 us)
Sparse Core Ops, SparseCore 0:
  41.8 23.0 all-gather.11
  66.4 17.4 all-gather.15
  86.0 24.0 all-gather.13
  132.8 32.8 reduce-scatter.15
  177.2 24.0 all-gather.17
  214.8 32.8 reduce-scatter.17
  257.9 24.0 all-gather.19
  285.4 70.5 reduce-scatter.27
  359.4 63.8 reduce-scatter.23
  426.5 63.8 reduce-scatter.25
  492.9 31.7 reduce-scatter.19
  528.0 70.9 reduce-scatter.21
